TPU v7x, 32 devices: a whole 2x2x4 slice. The times are simulated.
32 devices in a mesh: group: 2 (over y), wide: 8 (over z, x), narrow: 2 (over core).
Axes of the slice: x: 2, y: 2, z: 4, core: 2. Of those that a mesh axis runs over, the one named last changes fastest.
Arguments:
- hidden_in: bfloat16 [16, 16384], P(('group', 'wide'), 'narrow'), parts along dimension 0, may hold values from -60 to 60
- norm_gain: float32 [16384], P('narrow'), may hold values from 0.1 to 1.9
- qkv_weight: bfloat16 [16384, 9216], P('narrow', 'wide'), may hold values from -0.046875 to 0.046875
- out_weight: bfloat16 [8192, 16384], P('narrow', 'wide'), may hold values from -0.25 to 0.25
- cache_keys: bfloat16 [16, 256, 512], P(('group', 'wide'), None, 'narrow'), parts along dimension 0, may hold values from -500 to 500
- cache_values: bfloat16 [16, 256, 512], P(('group', 'wide'), None, 'narrow'), parts along dimension 0, may hold values from -6 to 6
- cache_lengths: int32 [16], P(('group', 'wide')), parts along dimension 0, may hold values from 4 to 256, as said below
Outputs:
- layer_out: float32 [16, 16384], P(('group', 'wide'), 'narrow'), parts along dimension 0
There are 2 independent parts, one for each index of `group`. A program takes and returns all parts, laid end to end along the dimension named above; an argument that names none is the same for every part. Nothing has to cross between parts.
Inputs may be any that keep to these rules, and one draw needn't show every extreme that they name: Some row's length is exactly 256 in every draw; row r's cached positions are 0 to cache_lengths[r] - 1 and its new token stands at position cache_lengths[r].
All inputs are finite; a program needn't handle non-finite values.
Results may differ from a plain program's by a relative error of at most 0.0058.
Values may be sent and summed in bfloat16 or wider, within the bound.
No kernel may reach another device: no remote copies, remote signals or barrier semaphores. Data moves between devices by JAX's collectives and lax.ppermute only.
A program may use at most 64 MiB of HBM per device.

v0:
```python
import jax
import jax.numpy as jnp
from jax import lax
from jax.sharding import PartitionSpec as P

D = 16384
HD = 128
rope_theta = 500000.0
norm_eps = 1e-05


def rotary(values, position):
    half = values.shape[-1] // 2
    frequency = rope_theta ** (-jnp.arange(half, dtype=jnp.float32) * 2.0 / values.shape[-1])
    angles = position[..., None] * frequency
    cosine = jnp.cos(angles)
    sine = jnp.sin(angles)
    first = values[..., :half]
    second = values[..., half:]
    return jnp.concatenate([first * cosine - second * sine, second * cosine + first * sine], -1)


def attend(joined, keys, values, lengths):
    count = joined.shape[0]
    groups = joined.shape[1]
    share = joined.shape[2] - 2
    head_dim = joined.shape[3]
    capacity = keys.shape[1]
    position = lengths.astype(jnp.float32)
    query = (rotary(joined[:, :, :share], position[:, None, None]) * head_dim ** (-0.5)).astype(
        jnp.bfloat16
    )
    new_key = rotary(joined[:, :, share], position[:, None]).astype(jnp.bfloat16)
    new_value = joined[:, :, share + 1].astype(jnp.bfloat16)
    keys_four = keys.reshape(count, capacity, groups, head_dim)
    values_four = values.reshape(count, capacity, groups, head_dim)
    scores = jnp.einsum("bgjd,btgd->bgjt", query, keys_four, preferred_element_type=jnp.float32)
    own = jnp.sum(query.astype(jnp.float32) * new_key.astype(jnp.float32)[:, :, None, :], -1)
    live = jnp.arange(capacity)[None, None, None, :] < lengths[:, None, None, None]
    scores = jnp.where(live, scores, -1e30)
    top = jnp.maximum(jnp.max(scores, -1), own)
    expo = jnp.exp(scores - top[..., None])
    own_expo = jnp.exp(own - top)
    total = jnp.sum(expo, -1) + own_expo
    probs = (expo / total[..., None]).astype(jnp.bfloat16)
    mixed = jnp.einsum("bgjt,btgd->bgjd", probs, values_four, preferred_element_type=jnp.float32)
    mixed = mixed + (own_expo / total)[..., None] * new_value.astype(jnp.float32)[:, :, None, :]
    return mixed.astype(jnp.bfloat16).reshape(count, groups * share * head_dim)


def body(hidden_in, norm_gain, qkv_weight, out_weight, cache_keys, cache_values, cache_lengths):
    inputs = hidden_in.astype(jnp.float32)
    row_count = hidden_in.shape[0]
    squares = lax.psum(jnp.sum(inputs * inputs, -1), "narrow")
    normed = (inputs * lax.rsqrt(squares / D + norm_eps)[:, None] * norm_gain).astype(jnp.bfloat16)
    partial_qkv = jnp.dot(
        lax.all_gather(normed, "wide", axis=0, tiled=True),
        qkv_weight,
        preferred_element_type=jnp.float32,
    )
    all_rows, col_block = partial_qkv.shape
    halves = partial_qkv.reshape(all_rows, 1, 2, col_block // 2)
    paired = lax.psum_scatter(halves, "narrow", scatter_dimension=2, tiled=True)
    moved = lax.all_to_all(paired, "wide", split_axis=0, concat_axis=1, tiled=True)
    blocks = moved.shape[1]
    parted = moved.reshape(row_count, 2, blocks // 2, 1, col_block // 2)
    owned = lax.all_to_all(parted, "narrow", split_axis=1, concat_axis=3, tiled=True)
    owned = owned.reshape(row_count, blocks // 2 * col_block)
    groups = cache_keys.shape[2] // HD
    owned = owned.reshape(row_count, groups, owned.shape[1] // (groups * HD), HD)
    mixed = attend(owned, cache_keys, cache_values, cache_lengths)
    partial_out = jnp.dot(
        lax.all_gather(mixed, "wide", axis=0, tiled=True),
        out_weight,
        preferred_element_type=jnp.float32,
    )
    all_rows, col_block = partial_out.shape
    halves = partial_out.reshape(all_rows, 1, 2, col_block // 2)
    paired = lax.psum_scatter(halves, "narrow", scatter_dimension=2, tiled=True)
    moved = lax.all_to_all(paired, "wide", split_axis=0, concat_axis=1, tiled=True)
    blocks = moved.shape[1]
    parted = moved.reshape(row_count, 2, blocks // 2, 1, col_block // 2)
    added = lax.all_to_all(parted, "narrow", split_axis=1, concat_axis=3, tiled=True)
    added = added.reshape(row_count, blocks // 2 * col_block)
    return inputs + added


def solution(mesh):
    placed = (
        P(("group", "wide"), "narrow"),
        P("narrow"),
        P("narrow", "wide"),
        P("narrow", "wide"),
        P(("group", "wide"), None, "narrow"),
        P(("group", "wide"), None, "narrow"),
        P(("group", "wide")),
    )
    return jax.shard_map(
        body, mesh=mesh, in_specs=placed, out_specs=P(("group", "wide"), "narrow"), check_vma=False
    )
```

profile of v0, /device:TPU:0, one launch (start us, length us, event | category | flops | bytes accessed | tf_op | source)
XLA Modules:
  0.0 149.4 jit_solution(13513085413637469094)
XLA Ops:
  6.5 1.5 multiply_reduce_fusion
  8.0 3.2 %psum.7 = f32[1]{0:T(128)} all-reduce(f32[1]{0:T(128)} %bitcast.1), channel_id=1, replica_groups=mesh['group'=2,'wide'=8,'narrow'=2] {'narrow'}, use_global_device_ids=true, to_apply=%region_1.0 | all-reduce | flops 1 | bytes 8 | tf_op jit(solution)/shard_map/psum | solution.py:54
  11.9 0.8 convert_bitcast_fusion
  12.8 32.4 %all-gather = bf16[8,1,8192]{2,1,0:T(2,128)(2,1)S(1)} all-gather(bf16[1,1,8192]{2,1,0:T(2,128)(2,1)S(1)} %convert_bitcast_fusion), channel_id=1, replica_groups=mesh['group'=2,'wide'=8,'narrow'=2] {'wide'}, dimensions={0}, use_global_device_ids=true | all-gather | bytes 147456 | tf_op jit(solution)/shard_map/all_gather | solution.py:57
  45.2 7.7 %fusion.1 = f32[8,1152]{1,0:T(8,128)S(1)} fusion(bf16[8192,1152]{1,0:T(8,128)(2,1)} %param.9, bf16[8,1,8192]{2,1,0:T(2,128)(2,1)S(1)} %all-gather), kind=kOutput, calls=%fused_computation.3 | convolution fusion | flops 150994944 | bytes 19042304 | tf_op jit(solution)/shard_map/dot_general | solution.py:56
  52.9 0.1 reshape.240
  53.0 0.6 copy.38
  54.3 7.9 %reduce-scatter.8.cloned.1.call-done = f32[8,1,1,576]{3,0,1,2:T(8,128)} async-done(((f32[8,1,2,576]{3,0,1,2:T(8,128)}), f32[8,1,1,576]{3,0,1,2:T(8,128)}) %reduce-scatter.8.cloned.1.call-update) | async-done | bytes 18448
  62.2 1.4 copy.39
  63.6 5.7 %all-to-all-start = ((f32[8,1,1,576]{3,2,1,0:T(1,128)}), f32[8,1,1,576]{3,2,1,0:T(1,128)S(1)}, u32[]{:S(2)}, u32[]{:S(2)}) async-start(f32[8,1,1,576]{3,2,1,0:T(1,128)} %copy.39), calls=%async_computation | async-start | bytes 40960 | tf_op jit(solution)/shard_map/all_to_all | solution.py:64
  69.4 6.4 %all-to-all-done = f32[8,1,1,576]{3,2,1,0:T(1,128)S(1)} async-done(((f32[8,1,1,576]{3,2,1,0:T(1,128)}), f32[8,1,1,576]{3,2,1,0:T(1,128)S(1)}, u32[]{:S(2)}, u32[]{:S(2)}) %all-to-all-start) | async-done | bytes 18464 | tf_op jit(solution)/shard_map/all_to_all | solution.py:64
  75.9 3.7 %all_to_all.48 = f32[1,2,4,1,576]{4,3,2,0,1:T(1,128)S(1)} all-to-all(f32[1,2,4,1,576]{4,3,2,0,1:T(1,128)S(1)} %bitcast.47), channel_id=1, replica_groups=mesh['group'=2,'wide'=8,'narrow'=2] {'narrow'}, dimensions={1} | all-to-all | bytes 36864 | tf_op jit(solution)/shard_map/all_to_all | solution.py:67
  79.6 0.1 reshape_reshape.3
  79.9 0.2 multiply_reduce_fusion.1
  80.1 0.3 fusion.25
  80.4 0.2 fusion.9
  80.6 0.2 fusion
  80.8 30.6 %all-gather.1 = bf16[8,1,4096]{2,1,0:T(2,128)(2,1)S(1)} all-gather(bf16[1,1,4096]{2,1,0:T(2,128)(2,1)S(1)} %reshape.251), channel_id=1, replica_groups=mesh['group'=2,'wide'=8,'narrow'=2] {'wide'}, dimensions={0}, use_global_device_ids=true | all-gather | bytes 73728 | tf_op jit(solution)/shard_map/all_gather | solution.py:73
  111.4 8.7 %fusion.6 = f32[8,2048]{1,0:T(8,128)} fusion(bf16[4096,2048]{1,0:T(8,128)(2,1)} %param.10, bf16[8,1,4096]{2,1,0:T(2,128)(2,1)S(1)} %all-gather.1), kind=kOutput, calls=%fused_computation.8 | convolution fusion | flops 134217728 | bytes 16908288 | tf_op jit(solution)/shard_map/dot_general | solution.py:72
  120.1 5.0 %reduce-scatter.6.cloned.1.call-done = f32[8,1,1,1024]{3,0,1,2:T(8,128)} async-done(((f32[8,1,2,1024]{3,0,1,2:T(8,128)}), f32[8,1,1,1024]{3,0,1,2:T(8,128)}) %reduce-scatter.6.cloned.1.call-update) | async-done | bytes 32784 | tf_op jit(solution)/shard_map/reduce_scatter | solution.py:79
  125.1 0.8 copy.45
  125.9 12.2 %all_to_all.49 = f32[8,1,1,1024]{3,2,1,0:T(1,128)S(1)} all-to-all(f32[8,1,1,1024]{3,2,1,0:T(1,128)S(1)} %copy.45), channel_id=1, replica_groups=mesh['group'=2,'wide'=8,'narrow'=2] {'wide'}, dimensions={0} | all-to-all | bytes 65536 | tf_op jit(solution)/shard_map/all_to_all | solution.py:80
  138.1 3.7 %all_to_all.50 = f32[1,2,4,1,1024]{4,2,3,0,1:T(4,128)S(1)} all-to-all(f32[1,2,4,1,1024]{4,2,3,0,1:T(4,128)S(1)} %copy.46), channel_id=1, replica_groups=mesh['group'=2,'wide'=8,'narrow'=2] {'narrow'}, dimensions={1} | all-to-all | bytes 65536 | tf_op jit(solution)/shard_map/all_to_all | solution.py:83
  141.9 0.7 convert_add_fusion
  (26 shorter events, 0.6 us)
Async XLA Ops:
  6.5 62.8 %copy-start.1 = (bf16[1,256,256]{2,1,0:T(8,128)(2,1)S(1)}, bf16[1,256,256]{2,1,0:T(8,128)(2,1)}, u32[]{:S(2)}) copy-start(bf16[1,256,256]{2,1,0:T(8,128)(2,1)} %param.11) | copy-start | bytes 393220
  6.5 62.9 %copy-start.2 = (bf16[1,256,256]{2,1,0:T(8,128)(2,1)S(1)}, bf16[1,256,256]{2,1,0:T(8,128)(2,1)}, u32[]{:S(2)}) copy-start(bf16[1,256,256]{2,1,0:T(8,128)(2,1)} %param.12) | copy-start | bytes 393220
  6.5 55.7 %reduce-scatter.8.cloned.1.call-start = ((), (), s32[]{:S(2)}) async-start(), calls=%async_computation.7 | async-start | bytes 61440
  52.9 89.0 %copy-start = (bf16[1,8192]{1,0:T(2,128)(2,1)S(1)}, bf16[1,8192]{1,0:T(2,128)(2,1)}, u32[]{:S(2)}) copy-start(bf16[1,8192]{1,0:T(2,128)(2,1)} %param.7) | copy-start | bytes 49156
  63.6 12.3 %all-to-all-start = ((f32[8,1,1,576]{3,2,1,0:T(1,128)}), f32[8,1,1,576]{3,2,1,0:T(1,128)S(1)}, u32[]{:S(2)}, u32[]{:S(2)}) async-start(f32[8,1,1,576]{3,2,1,0:T(1,128)} %copy.39), calls=%async_computation | async-start | bytes 40960 | tf_op jit(solution)/shard_map/all_to_all | solution.py:64
  69.3 55.8 %reduce-scatter.6.cloned.1.call-start = ((), (), s32[]{:S(2)}) async-start(), calls=%async_computation.6 | async-start | bytes 98304 | tf_op jit(solution)/shard_map/reduce_scatter | solution.py:79
Sparse Core Ops, SparseCore 0:
  53.7 8.4 reduce-scatter.7
  120.2 4.7 reduce-scatter.5
where the time goes:
time: 150 us; the launch traced here: 149 us
  blocking collectives  85.9 us (57%)
  waiting for transfers between devices  19.3 us (13%)
  matrix products  16.9 us (11%)
  between operations  14.8 us (10%)
  starting transfers between devices  5.74 us (4%)
  other arithmetic  3.6 us (2%)
  local copies, waits for them, and re-layouts  3.14 us (2%)
    all_gather x1, blocking collectives, body(): lax.all_gather(normed, 'wide', axis=0, tiled=True)  32.4 us
    all_gather x1, blocking collectives, body(): lax.all_gather(mixed, 'wide', axis=0, tiled=True)  30.6 us
    all_to_all x1, blocking collectives, body(): lax.all_to_all(paired, 'wide', split_axis=0, concat_axis=1, tiled=True)  12.2 us
    dot_general x1, matrix products, body(): jnp.dot(lax.all_gather(mixed, 'wide', axis=0, tiled=True), out_weight, pr...  8.68 us
    unnamed x3, waiting for transfers between devices  7.94 us
    dot_general x1, matrix products, body(): jnp.dot(lax.all_gather(normed, 'wide', axis=0, tiled=True), qkv_weight, p...  7.71 us
    all_to_all x2, blocking collectives, body(): lax.all_to_all(parted, 'narrow', split_axis=1, concat_axis=3, tiled=True)  7.46 us
    all_to_all x1, waiting for transfers between devices, body(): lax.all_to_all(paired, 'wide', split_axis=0, concat_axis=1, tiled=True)  6.45 us
  transfers between devices with their start and end apart: 3, of which 3 were waited for; matrix products, arithmetic and copies ran while one was open for 0% of the time, Pallas kernels for 0%

commit v1 on v0

--- a/solution.py
+++ b/solution.py
@@ -1,3 +1,4 @@
+import functools
 import jax
 import jax.numpy as jnp
 from jax import lax
@@ -7,6 +8,37 @@
 HD = 128
 rope_theta = 500000.0
 norm_eps = 1e-05
+
+
+def ladders_work(raw, along_dim):
+    t1 = lax.axis_size("wide")
+    outcome_arr, wide_out, carry = (t1, lax.axis_index("wide"), raw.shape[along_dim])
+    rack = []
+    for i in range(outcome_arr):
+        rack.append((i, (i + 1) % outcome_arr))
+    trail = []
+    for i in range(outcome_arr):
+        trail.append((i, (i - 1) % outcome_arr))
+    y_new = jnp.zeros(
+        (*raw.shape[:along_dim], outcome_arr * carry, *raw.shape[along_dim + 1 :]), raw.dtype
+    )
+    y_new = lax.dynamic_update_slice_in_dim(y_new, raw, wide_out * carry, axis=along_dim)
+    current_arr = v_now = raw
+    mid_arr = outcome_arr // 2
+    for c in range(1, mid_arr + 1):
+        current_arr = lax.ppermute(current_arr, axis_name="wide", perm=rack)
+        y_new = lax.dynamic_update_slice_in_dim(
+            y_new, current_arr, (wide_out - c) % outcome_arr * carry, axis=along_dim
+        )
+        if c < outcome_arr - mid_arr:
+            v_now = lax.ppermute(v_now, axis_name="wide", perm=trail)
+            y_new = lax.dynamic_update_slice_in_dim(
+                y_new, v_now, (wide_out + c) % outcome_arr * carry, axis=along_dim
+            )
+    return y_new
+
+
+connect_screen = functools.partial(ladders_work, along_dim=0)
 
 
 def rotary(values, position):
@@ -69,11 +101,7 @@
     groups = cache_keys.shape[2] // HD
     owned = owned.reshape(row_count, groups, owned.shape[1] // (groups * HD), HD)
     mixed = attend(owned, cache_keys, cache_values, cache_lengths)
-    partial_out = jnp.dot(
-        lax.all_gather(mixed, "wide", axis=0, tiled=True),
-        out_weight,
-        preferred_element_type=jnp.float32,
-    )
+    partial_out = jnp.dot(connect_screen(mixed), out_weight, preferred_element_type=jnp.float32)
     all_rows, col_block = partial_out.shape
     halves = partial_out.reshape(all_rows, 1, 2, col_block // 2)
     paired = lax.psum_scatter(halves, "narrow", scatter_dimension=2, tiled=True)

time: 150 us -> 145 us (0.967)
  blocking collectives: 85.9 us -> 55.3 us
  starting transfers between devices: 5.74 us -> 20 us
  waiting for transfers between devices: 19.3 us -> 29.2 us
  local copies, waits for them, and re-layouts: 3.14 us -> 4.92 us
    all_gather x1 -> x0, blocking collectives: 30.6 us -> none  [body(): lax.all_gather(mixed, 'wide', axis=0, tiled=True)]
    ppermute x0 -> x7, starting transfers between devices: none -> 14.2 us  [the longest x3 13.7 us: ladders_work(): v_now = lax.ppermute(v_now, axis_name='wide', perm=trail)]
    ppermute x0 -> x7, waiting for transfers between devices: none -> 9.91 us  [the longest x4 9.9 us: ladders_work(): current_arr = lax.ppermute(current_arr, axis_name='wide', perm=rack)]
    dynamic_update_slice x0 -> x8, local copies, waits for them, and re-layouts: none -> 1.77 us  [the longest x4 0.87 us: ladders_work(): lax.dynamic_update_slice_in_dim(y_new, current_arr, (wide_out - c) % outc...]
  transfers between devices with their start and end apart: 3 -> 10, of which waited for: 3 -> 7; matrix products, arithmetic and copies ran while one was open for 0% -> 1% of each run, Pallas kernels for 0% -> 0%
where the time goes in v1:
time: 145 us
  blocking collectives  55.3 us (38%)
  waiting for transfers between devices  29.2 us (20%)
  starting transfers between devices  20 us (14%)
  matrix products  16.8 us (12%)
  between operations  14.9 us (10%)
  local copies, waits for them, and re-layouts  4.92 us (3%)
  other arithmetic  3.6 us (2%)
    all_gather x1, blocking collectives, body(): lax.all_gather(normed, 'wide', axis=0, tiled=True)  32.4 us
    ppermute x3, starting transfers between devices, ladders_work(): v_now = lax.ppermute(v_now, axis_name='wide', perm=trail)  13.7 us
    all_to_all x1, blocking collectives, body(): lax.all_to_all(paired, 'wide', split_axis=0, concat_axis=1, tiled=True)  12.2 us
    ppermute x4, waiting for transfers between devices, ladders_work(): current_arr = lax.ppermute(current_arr, axis_name='wide', perm=rack)  9.9 us
    dot_general x1, matrix products, body(): jnp.dot(connect_screen(mixed), out_weight, preferred_element_type=jnp.flo...  8.66 us
    unnamed x3, waiting for transfers between devices  7.94 us
    dot_general x1, matrix products, body(): jnp.dot(lax.all_gather(normed, 'wide', axis=0, tiled=True), qkv_weight, p...  7.71 us
    all_to_all x2, blocking collectives, body(): lax.all_to_all(parted, 'narrow', split_axis=1, concat_axis=3, tiled=True)  7.46 us
  transfers between devices with their start and end apart: 10, of which 7 were waited for; matrix products, arithmetic and copies ran while one was open for 1% of the time, Pallas kernels for 0%

profile of v1, /device:TPU:0, one launch (start us, length us, event | category | flops | bytes accessed | tf_op | source)
XLA Modules:
  0.0 144.8 jit_solution(13440198395515562684)
XLA Ops:
  6.5 1.5 %multiply_reduce_fusion = f32[]{:T(128)} fusion(bf16[1,8192]{1,0:T(2,128)(2,1)} %param.7), kind=kLoop, calls=%fused_computation.11 | loop fusion | flops 24575 | bytes 16388 | tf_op jit(solution)/shard_map/reduce_sum | solution.py:86
  8.0 3.2 %psum.7 = f32[1]{0:T(128)} all-reduce(f32[1]{0:T(128)} %bitcast.1), channel_id=1, replica_groups=mesh['group'=2,'wide'=8,'narrow'=2] {'narrow'}, use_global_device_ids=true, to_apply=%region_1.0 | all-reduce | flops 1 | bytes 8 | tf_op jit(solution)/shard_map/psum | solution.py:86
  11.9 0.8 convert_bitcast_fusion
  12.8 32.4 %all-gather = bf16[8,1,8192]{2,1,0:T(2,128)(2,1)S(1)} all-gather(bf16[1,1,8192]{2,1,0:T(2,128)(2,1)S(1)} %convert_bitcast_fusion), channel_id=1, replica_groups=mesh['group'=2,'wide'=8,'narrow'=2] {'wide'}, dimensions={0}, use_global_device_ids=true | all-gather | bytes 147456 | tf_op jit(solution)/shard_map/all_gather | solution.py:89
  45.2 7.7 %fusion.1 = f32[8,1152]{1,0:T(8,128)S(1)} fusion(bf16[8192,1152]{1,0:T(8,128)(2,1)} %param.9, bf16[8,1,8192]{2,1,0:T(2,128)(2,1)S(1)} %all-gather), kind=kOutput, calls=%fused_computation.3 | convolution fusion | flops 150994944 | bytes 19042304 | tf_op jit(solution)/shard_map/dot_general | solution.py:88
  53.0 0.6 copy.36
  54.3 7.9 %reduce-scatter.8.cloned.1.call-done = f32[8,1,1,576]{3,0,1,2:T(8,128)} async-done(((f32[8,1,2,576]{3,0,1,2:T(8,128)}), f32[8,1,1,576]{3,0,1,2:T(8,128)}) %reduce-scatter.8.cloned.1.call-update) | async-done | bytes 18448
  62.2 1.4 copy.37
  63.6 5.7 %all-to-all-start = ((f32[8,1,1,576]{3,2,1,0:T(1,128)}), f32[8,1,1,576]{3,2,1,0:T(1,128)S(1)}, u32[]{:S(2)}, u32[]{:S(2)}) async-start(f32[8,1,1,576]{3,2,1,0:T(1,128)} %copy.37), calls=%async_computation | async-start | bytes 40960 | tf_op jit(solution)/shard_map/all_to_all | solution.py:96
  69.4 6.4 %all-to-all-done = f32[8,1,1,576]{3,2,1,0:T(1,128)S(1)} async-done(((f32[8,1,1,576]{3,2,1,0:T(1,128)}), f32[8,1,1,576]{3,2,1,0:T(1,128)S(1)}, u32[]{:S(2)}, u32[]{:S(2)}) %all-to-all-start) | async-done | bytes 18464 | tf_op jit(solution)/shard_map/all_to_all | solution.py:96
  75.9 3.7 %all_to_all.48 = f32[1,2,4,1,576]{4,3,2,0,1:T(1,128)S(1)} all-to-all(f32[1,2,4,1,576]{4,3,2,0,1:T(1,128)S(1)} %bitcast.45), channel_id=1, replica_groups=mesh['group'=2,'wide'=8,'narrow'=2] {'narrow'}, dimensions={1} | all-to-all | bytes 36864 | tf_op jit(solution)/shard_map/all_to_all | solution.py:99
  81.4 4.2 %collective-permute-start.1 = (bf16[1,4096]{1,0:T(2,128)(2,1)S(1)}, bf16[1,4096]{1,0:T(2,128)(2,1)S(1)}, u32[]{:S(2)}, u32[]{:S(2)}) collective-permute-start(bf16[1,4096]{1,0:T(2,128)(2,1)S(1)} %reshape.244), channel_id=1, source_target_pairs={{0,14},{2,0},{4,2},{6,4},{8,6},{10,8},{12,10},{14,12},{1,15},{3,1}... | collective-permute-start | bytes 24584 | tf_op jit(solution)/shard_map/ppermute | solution.py:34
  85.6 1.7 %collective-permute-done = bf16[1,4096]{1,0:T(2,128)(2,1)S(1)} collective-permute-done((bf16[1,4096]{1,0:T(2,128)(2,1)S(1)}, bf16[1,4096]{1,0:T(2,128)(2,1)S(1)}, u32[]{:S(2)}, u32[]{:S(2)}) %collective-permute-start) | collective-permute-done | bytes 8224 | tf_op jit(solution)/shard_map/ppermute | solution.py:29
  87.3 4.7 %collective-permute-start.3 = (bf16[1,4096]{1,0:T(2,128)(2,1)S(1)}, bf16[1,4096]{1,0:T(2,128)(2,1)S(1)}, u32[]{:S(2)}, u32[]{:S(2)}) collective-permute-start(bf16[1,4096]{1,0:T(2,128)(2,1)S(1)} %collective-permute-done.1), channel_id=1, source_target_pairs={{0,14},{2,0},{4,2},{6,4},{8,6},{10,8},{12,10},{14,12},{1,15},{3,1}... | collective-permute-start | bytes 24584 | tf_op jit(solution)/shard_map/ppermute | solution.py:34
  92.0 1.7 %collective-permute-done.2 = bf16[1,4096]{1,0:T(2,128)(2,1)S(1)} collective-permute-done((bf16[1,4096]{1,0:T(2,128)(2,1)S(1)}, bf16[1,4096]{1,0:T(2,128)(2,1)S(1)}, u32[]{:S(2)}, u32[]{:S(2)}) %collective-permute-start.2) | collective-permute-done | bytes 8224 | tf_op jit(solution)/shard_map/ppermute | solution.py:29
  93.7 4.7 %collective-permute-start.5 = (bf16[1,4096]{1,0:T(2,128)(2,1)S(1)}, bf16[1,4096]{1,0:T(2,128)(2,1)S(1)}, u32[]{:S(2)}, u32[]{:S(2)}) collective-permute-start(bf16[1,4096]{1,0:T(2,128)(2,1)S(1)} %collective-permute-done.3), channel_id=1, source_target_pairs={{0,14},{2,0},{4,2},{6,4},{8,6},{10,8},{12,10},{14,12},{1,15},{3,1}... | collective-permute-start | bytes 24584 | tf_op jit(solution)/shard_map/ppermute | solution.py:34
  98.5 1.7 %collective-permute-done.4 = bf16[1,4096]{1,0:T(2,128)(2,1)S(1)} collective-permute-done((bf16[1,4096]{1,0:T(2,128)(2,1)S(1)}, bf16[1,4096]{1,0:T(2,128)(2,1)S(1)}, u32[]{:S(2)}, u32[]{:S(2)}) %collective-permute-start.4) | collective-permute-done | bytes 8224 | tf_op jit(solution)/shard_map/ppermute | solution.py:29
  101.8 4.8 %collective-permute-done.6 = bf16[1,4096]{1,0:T(2,128)(2,1)S(1)} collective-permute-done((bf16[1,4096]{1,0:T(2,128)(2,1)S(1)}, bf16[1,4096]{1,0:T(2,128)(2,1)S(1)}, u32[]{:S(2)}, u32[]{:S(2)}) %collective-permute-start.6) | collective-permute-done | bytes 8224 | tf_op jit(solution)/shard_map/ppermute | solution.py:29
  106.8 8.7 %fusion.23 = f32[8,2048]{1,0:T(8,128)} fusion(bf16[8,4096]{1,0:T(8,128)(2,1)S(1)} %dynamic_update_slice.31, bf16[4096,2048]{1,0:T(8,128)(2,1)} %param.10), kind=kOutput, calls=%fused_computation.41 | convolution fusion | flops 134217728 | bytes 16908288 | tf_op jit(solution)/shard_map/dot_general | solution.py:104
  115.5 5.0 %reduce-scatter.6.cloned.1.call-done = f32[8,1,1,1024]{3,0,1,2:T(8,128)} async-done(((f32[8,1,2,1024]{3,0,1,2:T(8,128)}), f32[8,1,1,1024]{3,0,1,2:T(8,128)}) %reduce-scatter.6.cloned.1.call-update) | async-done | bytes 32784 | tf_op jit(solution)/shard_map/reduce_scatter | solution.py:107
  120.4 0.8 copy.43
  121.2 12.2 %all_to_all.49 = f32[8,1,1,1024]{3,2,1,0:T(1,128)S(1)} all-to-all(f32[8,1,1,1024]{3,2,1,0:T(1,128)S(1)} %copy.43), channel_id=1, replica_groups=mesh['group'=2,'wide'=8,'narrow'=2] {'wide'}, dimensions={0} | all-to-all | bytes 65536 | tf_op jit(solution)/shard_map/all_to_all | solution.py:108
  133.4 3.7 %all_to_all.50 = f32[1,2,4,1,1024]{4,2,3,0,1:T(4,128)S(1)} all-to-all(f32[1,2,4,1,1024]{4,2,3,0,1:T(4,128)S(1)} %copy.44), channel_id=1, replica_groups=mesh['group'=2,'wide'=8,'narrow'=2] {'narrow'}, dimensions={1} | all-to-all | bytes 65536 | tf_op jit(solution)/shard_map/all_to_all | solution.py:111
  137.3 0.7 convert_add_fusion
  (48 shorter events, 3.9 us)
Async XLA Ops:
  6.5 62.8 %copy-start.1 = (bf16[1,256,256]{2,1,0:T(8,128)(2,1)S(1)}, bf16[1,256,256]{2,1,0:T(8,128)(2,1)}, u32[]{:S(2)}) copy-start(bf16[1,256,256]{2,1,0:T(8,128)(2,1)} %param.11) | copy-start | bytes 393220
  6.5 62.9 %copy-start.2 = (bf16[1,256,256]{2,1,0:T(8,128)(2,1)S(1)}, bf16[1,256,256]{2,1,0:T(8,128)(2,1)}, u32[]{:S(2)}) copy-start(bf16[1,256,256]{2,1,0:T(8,128)(2,1)} %param.12) | copy-start | bytes 393220
  6.5 55.7 %reduce-scatter.8.cloned.1.call-start = ((), (), s32[]{:S(2)}) async-start(), calls=%async_computation.7 | async-start | bytes 61440
  52.9 84.4 %copy-start = (bf16[1,8192]{1,0:T(2,128)(2,1)S(1)}, bf16[1,8192]{1,0:T(2,128)(2,1)}, u32[]{:S(2)}) copy-start(bf16[1,8192]{1,0:T(2,128)(2,1)} %param.7) | copy-start | bytes 49156
  63.6 12.3 %all-to-all-start = ((f32[8,1,1,576]{3,2,1,0:T(1,128)}), f32[8,1,1,576]{3,2,1,0:T(1,128)S(1)}, u32[]{:S(2)}, u32[]{:S(2)}) async-start(f32[8,1,1,576]{3,2,1,0:T(1,128)} %copy.37), calls=%async_computation | async-start | bytes 40960 | tf_op jit(solution)/shard_map/all_to_all | solution.py:96
  69.3 51.1 %reduce-scatter.6.cloned.1.call-start = ((), (), s32[]{:S(2)}) async-start(), calls=%async_computation.6 | async-start | bytes 98304 | tf_op jit(solution)/shard_map/reduce_scatter | solution.py:107
  80.8 6.5 %collective-permute-start = (bf16[1,4096]{1,0:T(2,128)(2,1)S(1)}, bf16[1,4096]{1,0:T(2,128)(2,1)S(1)}, u32[]{:S(2)}, u32[]{:S(2)}) collective-permute-start(bf16[1,4096]{1,0:T(2,128)(2,1)S(1)} %reshape.244), channel_id=1, source_target_pairs={{0,2},{2,4},{4,6},{6,8},{8,10},{10,12},{12,14},{14,0},{1,3},{3,5},... | collective-permute-start | bytes 24584 | tf_op jit(solution)/shard_map/ppermute | solution.py:29
  81.4 5.9 %collective-permute-start.1 = (bf16[1,4096]{1,0:T(2,128)(2,1)S(1)}, bf16[1,4096]{1,0:T(2,128)(2,1)S(1)}, u32[]{:S(2)}, u32[]{:S(2)}) collective-permute-start(bf16[1,4096]{1,0:T(2,128)(2,1)S(1)} %reshape.244), channel_id=1, source_target_pairs={{0,14},{2,0},{4,2},{6,4},{8,6},{10,8},{12,10},{14,12},{1,15},{3,1}... | collective-permute-start | bytes 24584 | tf_op jit(solution)/shard_map/ppermute | solution.py:34
  87.3 6.4 %collective-permute-start.2 = (bf16[1,4096]{1,0:T(2,128)(2,1)S(1)}, bf16[1,4096]{1,0:T(2,128)(2,1)S(1)}, u32[]{:S(2)}, u32[]{:S(2)}) collective-permute-start(bf16[1,4096]{1,0:T(2,128)(2,1)S(1)} %collective-permute-done), channel_id=1, source_target_pairs={{0,2},{2,4},{4,6},{6,8},{8,10},{10,12},{12,14},{14,0},{1,3},{3,5},... | collective-permute-start | bytes 24584 | tf_op jit(solution)/shard_map/ppermute | solution.py:29
  87.3 6.4 %collective-permute-start.3 = (bf16[1,4096]{1,0:T(2,128)(2,1)S(1)}, bf16[1,4096]{1,0:T(2,128)(2,1)S(1)}, u32[]{:S(2)}, u32[]{:S(2)}) collective-permute-start(bf16[1,4096]{1,0:T(2,128)(2,1)S(1)} %collective-permute-done.1), channel_id=1, source_target_pairs={{0,14},{2,0},{4,2},{6,4},{8,6},{10,8},{12,10},{14,12},{1,15},{3,1}... | collective-permute-start | bytes 24584 | tf_op jit(solution)/shard_map/ppermute | solution.py:34
  93.7 6.4 %collective-permute-start.4 = (bf16[1,4096]{1,0:T(2,128)(2,1)S(1)}, bf16[1,4096]{1,0:T(2,128)(2,1)S(1)}, u32[]{:S(2)}, u32[]{:S(2)}) collective-permute-start(bf16[1,4096]{1,0:T(2,128)(2,1)S(1)} %collective-permute-done.2), channel_id=1, source_target_pairs={{0,2},{2,4},{4,6},{6,8},{8,10},{10,12},{12,14},{14,0},{1,3},{3,5},... | collective-permute-start | bytes 24584 | tf_op jit(solution)/shard_map/ppermute | solution.py:29
  93.7 7.9 %collective-permute-start.5 = (bf16[1,4096]{1,0:T(2,128)(2,1)S(1)}, bf16[1,4096]{1,0:T(2,128)(2,1)S(1)}, u32[]{:S(2)}, u32[]{:S(2)}) collective-permute-start(bf16[1,4096]{1,0:T(2,128)(2,1)S(1)} %collective-permute-done.3), channel_id=1, source_target_pairs={{0,14},{2,0},{4,2},{6,4},{8,6},{10,8},{12,10},{14,12},{1,15},{3,1}... | collective-permute-start | bytes 24584 | tf_op jit(solution)/shard_map/ppermute | solution.py:34
  100.2 6.4 %collective-permute-start.6 = (bf16[1,4096]{1,0:T(2,128)(2,1)S(1)}, bf16[1,4096]{1,0:T(2,128)(2,1)S(1)}, u32[]{:S(2)}, u32[]{:S(2)}) collective-permute-start(bf16[1,4096]{1,0:T(2,128)(2,1)S(1)} %collective-permute-done.4), channel_id=1, source_target_pairs={{0,2},{2,4},{4,6},{6,8},{8,10},{10,12},{12,14},{14,0},{1,3},{3,5},... | collective-permute-start | bytes 24584 | tf_op jit(solution)/shard_map/ppermute | solution.py:29
Sparse Core Ops, SparseCore 0:
  53.7 8.4 reduce-scatter.7
  115.6 4.7 reduce-scatter.5
